TPU v7x, 32 devices: a whole 2x2x4 slice. The times are simulated.
32 devices in a mesh: snap: 8 (over z, y), ord: 4 (over x, core).
Axes of the slice: x: 2, y: 2, z: 4, core: 2. Of those that a mesh axis runs over, the one named last changes fastest.
Arguments:
- images: bfloat16 [512, 256, 1024], P(('snap', 'ord')), may hold values from -8 to 8
- cycle_masks: int32 [512, 256], P('snap'), may hold values from 0 to 1, as said below
- weights: float32 [512], P('snap'), may hold values from 1 to 4
- inversion: float32 [128, 128], replicated, may hold values from -1 to 2
Outputs:
- kam: float32 [128, 256, 256], P('ord', 'snap')
Inputs may be any that keep to these rules, and one draw needn't show every extreme that they name: `cycle_masks`: each entry is 0 or 1; the same 4 cycles, drawn from the seed, are 0 in every snapshot.
All inputs are finite; a program needn't handle non-finite values.
Results may differ from a plain program's by a relative error of at most 0.0015.
Values may be sent and summed in bfloat16 or wider, within the bound.
No kernel may reach another device: no remote copies, remote signals or barrier semaphores. Data moves between devices by JAX's collectives and lax.ppermute only.
A program may use at most 64 MiB of HBM per device.

v0:
```python
import math
import jax
import jax.numpy as jnp
from jax import lax
from jax.sharding import PartitionSpec as P


def make_table(orders, angles):
    order_index = jnp.arange(orders, dtype=jnp.int32)
    angle_index = jnp.arange(angles, dtype=jnp.int32)
    phase_index = order_index[:, None] * angle_index[None, :] % angles
    radians = phase_index.astype(jnp.float32) * (2.0 * math.pi / angles)
    norming = math.sqrt(2.0 / angles)
    return jnp.concatenate(
        [jnp.cos(radians) * norming, -jnp.sin(radians) * norming], axis=0
    ).astype(jnp.bfloat16)


def weighted_gram(arrived, weight_rows):
    weighted = (arrived.astype(jnp.float32) * weight_rows[None, None, :, None]).astype(jnp.bfloat16)
    return jnp.einsum("rlsq,rlsp->lqp", weighted, arrived, preferred_element_type=jnp.float32)


def on_device(images, cycle_masks, weights, inversion):
    snap_dev, cycle_count, angles = images.shape
    orders = inversion.shape[0]
    snap_size = lax.axis_size("snap")
    ord_size = lax.axis_size("ord")
    ord_index = lax.axis_index("ord")
    dft_table = make_table(orders, angles)
    group_masks = cycle_masks.astype(jnp.float32)
    own_masks = lax.dynamic_slice_in_dim(group_masks, ord_index * snap_dev, snap_dev, 0)
    coeffs = jnp.einsum("ka,sqa->ksq", dft_table, images, preferred_element_type=jnp.float32)
    coeffs = (
        (coeffs * own_masks[None]).astype(jnp.bfloat16).reshape(2, orders, snap_dev, cycle_count)
    )
    masked_weight = group_masks * weights[:, None]
    partial_count = jnp.einsum(
        "sq,sp->qp", masked_weight, group_masks, precision=lax.Precision.HIGHEST
    )
    per_device = orders // (snap_size * ord_size)
    shaped = coeffs.reshape(2, ord_size, snap_size * per_device, snap_dev, cycle_count)
    arrived = lax.all_to_all(
        lax.all_to_all(shaped, "snap", split_axis=2, concat_axis=3, tiled=True),
        "ord",
        split_axis=1,
        concat_axis=3,
        tiled=True,
    )
    arrived = arrived.reshape(2, per_device, -1, cycle_count)
    weight_all = lax.all_gather(weights, "snap", axis=0, tiled=True)
    weight_all = weight_all.reshape(snap_size, ord_size, snap_dev).transpose(1, 0, 2).reshape(-1)
    partial_value = weighted_gram(arrived, weight_all)
    gram_sum = lax.all_to_all(partial_value, "snap", split_axis=1, concat_axis=0, tiled=True)
    pair_count = lax.psum_scatter(partial_count, "snap", scatter_dimension=0, tiled=True)
    correl = gram_sum / jnp.maximum(pair_count, 1.0)[None]
    local_orders = correl.shape[0]
    own_rows = lax.dynamic_slice_in_dim(inversion, ord_index * local_orders, local_orders, 0)
    return jnp.einsum(
        "ln,nqp->lqp",
        own_rows,
        lax.all_gather(correl, "ord", axis=0, tiled=True),
        precision=lax.Precision.HIGHEST,
    )


def solution(mesh):
    placed = (P(("snap", "ord"), None, None), P("snap", None), P("snap"), P())
    return jax.shard_map(
        on_device, mesh=mesh, in_specs=placed, out_specs=P("ord", "snap", None), check_vma=False
    )
```

profile of v0, /device:TPU:0, one launch (start us, length us, event | category | flops | bytes accessed | tf_op | source)
XLA Modules:
  0.0 228.0 jit_solution(37374247902323197)
XLA Ops:
  6.5 2.2 multiply_convert_fusion.5
  8.7 0.8 convert_element_type.19
  9.6 5.8 %multiply_convert_fusion.1 = bf16[256,16,256]{2,0,1:T(8,128)(2,1)S(1)} fusion(bf16[16,256,1024]{2,1,0:T(8,128)(2,1)} %param.4, f32[16,256]{1,0:T(8,128)S(1)} %constant_dynamic-slice_fusion, bf16[128,1024]{1,0:T(8,128)(2,1)S(1)} %get-tuple-element.5, bf16[128,1024]{1,0:T(8,128)(2,1)S(1)} %get-tuple-element.6), kind=kOutput, calls=%fused_computation.1 | convolution fusion | flops 2150629376 | bytes 11026432 | tf_op jit(solution)/shard_map/ka,sqa->ksq/dot_general | solution.py:33
  15.3 1.6 copy.18
  17.0 55.3 %all_to_all.51 = bf16[2,4,32,16,256]{4,1,0,3,2:T(4,128)(2,1)S(1)} all-to-all(bf16[2,4,32,16,256]{4,1,0,3,2:T(4,128)(2,1)S(1)} %copy.18), channel_id=1, replica_groups=mesh['snap'=8,'ord'=4] {'snap'}, dimensions={2} | all-to-all | bytes 4194304 | tf_op jit(solution)/shard_map/all_to_all | solution.py:44
  72.3 1.8 copy.19
  74.1 3.6 %all-to-all-start.1 = ((bf16[2,4,4,128,256]{4,3,0,2,1:T(8,128)(2,1)}), bf16[2,4,4,128,256]{4,3,0,2,1:T(8,128)(2,1)S(1)}, u32[]{:S(2)}, u32[]{:S(2)}) async-start(bf16[2,4,4,128,256]{4,3,0,2,1:T(8,128)(2,1)} %bitcast.31), calls=%async_computation.1 | async-start | bytes 4194304 | tf_op jit(solution)/shard_map/all_to_all | solution.py:43
  77.8 0.6 dynamic-slice
  79.0 0.2 dynamic-update-slice
  79.3 19.4 %all-reduce = f32[512]{0:T(512)S(1)} all-reduce(f32[512]{0:T(512)S(1)} %dynamic-update-slice), channel_id=1, replica_groups=mesh['snap'=8,'ord'=4] {'snap'}, use_global_device_ids=true, to_apply=%add | all-reduce | flops 512 | bytes 4096
  98.7 0.1 reshape.12
  98.8 0.1 mul.76
  98.9 4.5 %all-to-all-done.1 = bf16[2,4,4,128,256]{4,3,0,2,1:T(8,128)(2,1)S(1)} async-done(((bf16[2,4,4,128,256]{4,3,0,2,1:T(8,128)(2,1)}), bf16[2,4,4,128,256]{4,3,0,2,1:T(8,128)(2,1)S(1)}, u32[]{:S(2)}, u32[]{:S(2)}) %all-to-all-start.1) | async-done | bytes 2097184 | tf_op jit(solution)/shard_map/all_to_all | solution.py:43
  103.4 0.1 copy.20
  103.5 0.0 copy-start.1
  103.5 1.2 fusion.2
  104.8 1.6 copy.23
  106.4 3.6 %all-to-all-start.2 = ((f32[4,256,256]{2,0,1:T(4,128)}), f32[4,256,256]{2,0,1:T(4,128)S(1)}, u32[]{:S(2)}, u32[]{:S(2)}) async-start(f32[4,256,256]{2,0,1:T(4,128)} %copy.23), calls=%async_computation.2 | async-start | bytes 2097152 | tf_op jit(solution)/shard_map/all_to_all | solution.py:54
  110.0 0.0 reduce-scatter.2.cloned.1.call-start
  110.1 1.2 fusion.11
  111.2 0.0 reduce-scatter.2.cloned.1.call-update
  111.3 0.0 all-gather.2.cloned.1.call-start
  111.3 68.1 %reduce-scatter.2.cloned.1.call-done = f32[32,256]{1,0:T(8,128)} async-done(((f32[256,256]{1,0:T(8,128)}), f32[32,256]{1,0:T(8,128)}) %reduce-scatter.2.cloned.1.call-update) | async-done | bytes 32784 | tf_op jit(solution)/shard_map/reduce_scatter | solution.py:55
  179.4 0.8 broadcast_maximum_fusion
  180.2 0.0 all-to-all-done.2
  180.2 0.3 copy.29
  180.5 0.4 all_to_all.47
  180.9 1.1 broadcast_divide_fusion
  181.9 0.0 all-gather.2.cloned.1.call-update
  182.0 33.6 %all-gather.2.cloned.1.call-done = f32[128,32,256]{2,0,1:T(8,128)} async-done(((f32[32,32,256]{2,0,1:T(8,128)}), f32[128,32,256]{2,0,1:T(8,128)}) %all-gather.2.cloned.1.call-update) | async-done | bytes 4194320 | tf_op jit(solution)/shard_map/all_gather | solution.py:62
  215.6 4.0 %fusion.14 = f32[32,32,256]{2,0,1:T(8,128)S(1)} fusion(f32[128,32,256]{2,0,1:T(8,128)} %all-gather.2.cloned.1.call-done, f32[128,128]{1,0:T(8,128)S(1)} %copy-done, s32[]{:T(128)S(6)} %select_n.15), kind=kOutput, calls=%fused_computation.24 | convolution fusion | flops 402653184 | bytes 5259268 | tf_op jit(solution)/shard_map/ln,nqp->lqp/dot_general | solution.py:59
  219.6 1.6 copy.25
  (10 shorter events, 0.0 us)
Async XLA Ops:
  6.5 209.1 %copy-start = (f32[128,128]{1,0:T(8,128)S(1)}, f32[128,128]{1,0:T(8,128)}, u32[]{:S(2)}) copy-start(f32[128,128]{1,0:T(8,128)} %param.7) | copy-start | bytes 196612
  72.3 5.4 %copy-start.3 = (u32[32]{0:T(128)S(1)}, u32[32]{0:T(128)}, u32[]{:S(2)}) copy-start(u32[32]{0:T(128)} %constant.37) | copy-start | bytes 388
  72.3 6.7 %copy-start.2 = (f32[64]{0:T(128)S(1)}, f32[64]{0:T(128)}, u32[]{:S(2)}) copy-start(f32[64]{0:T(128)} %param.6) | copy-start | bytes 772
  74.1 29.2 %all-to-all-start.1 = ((bf16[2,4,4,128,256]{4,3,0,2,1:T(8,128)(2,1)}), bf16[2,4,4,128,256]{4,3,0,2,1:T(8,128)(2,1)S(1)}, u32[]{:S(2)}, u32[]{:S(2)}) async-start(bf16[2,4,4,128,256]{4,3,0,2,1:T(8,128)(2,1)} %bitcast.31), calls=%async_computation.1 | async-start | bytes 4194304 | tf_op jit(solution)/shard_map/all_to_all | solution.py:43
  103.5 6.5 %copy-start.1 = (s32[64,256]{1,0:T(8,128)S(1)}, s32[64,256]{1,0:T(8,128)}, u32[]{:S(2)}) copy-start(s32[64,256]{1,0:T(8,128)} %param.5) | copy-start | bytes 196612
  106.4 73.8 %all-to-all-start.2 = ((f32[4,256,256]{2,0,1:T(4,128)}), f32[4,256,256]{2,0,1:T(4,128)S(1)}, u32[]{:S(2)}, u32[]{:S(2)}) async-start(f32[4,256,256]{2,0,1:T(4,128)} %copy.23), calls=%async_computation.2 | async-start | bytes 2097152 | tf_op jit(solution)/shard_map/all_to_all | solution.py:54
  110.0 69.4 %reduce-scatter.2.cloned.1.call-start = ((), (), s32[]{:S(2)}) async-start(), calls=%async_computation.4 | async-start | bytes 294912 | tf_op jit(solution)/shard_map/reduce_scatter | solution.py:55
  111.3 104.3 %all-gather.2.cloned.1.call-start = ((), (), s32[]{:S(2)}) async-start(), calls=%async_computation.5 | async-start | bytes 5242880 | tf_op jit(solution)/shard_map/all_gather | solution.py:62
Sparse Core Ops, SparseCore 0:
  114.1 65.2 reduce-scatter.1
  182.1 33.4 all-gather.1
where the time goes:
time: 228 us
  waiting for transfers between devices  106 us (46%)
  blocking collectives  74.8 us (33%)
  between operations  14.2 us (6%)
  matrix products  12.1 us (5%)
  local copies, waits for them, and re-layouts  8.48 us (4%)
  starting transfers between devices  7.28 us (3%)
  other arithmetic  4.87 us (2%)
    reduce_scatter x1, waiting for transfers between devices, on_device(): lax.psum_scatter(partial_count, 'snap', scatter_dimension=0, tiled=True)  68.1 us
    all_to_all x1, blocking collectives, on_device(): lax.all_to_all(shaped, 'snap', split_axis=2, concat_axis=3, tiled=True)  55.3 us
    all_gather x1, waiting for transfers between devices, on_device(): lax.all_gather(correl, 'ord', axis=0, tiled=True)  33.6 us
    unnamed x1, blocking collectives  19.4 us
    dot_general x1, matrix products, on_device(): jnp.einsum('ka,sqa->ksq', dft_table, images, preferred_element_type=jnp.f...  5.75 us
  transfers between devices with their start and end apart: 4, of which 3 were waited for; matrix products, arithmetic and copies ran while one was open for 1% of the time, Pallas kernels for 0%

commit v1 on v0

--- a/solution.py
+++ b/solution.py
@@ -3,6 +3,12 @@
 import jax.numpy as jnp
 from jax import lax
 from jax.sharding import PartitionSpec as P
+
+
+def trade_parts(x, name, split, join):
+    cells = jnp.split(x, lax.axis_size(name), axis=split)
+    received = lax.all_to_all(jnp.stack(cells), name, 0, 0)
+    return jnp.concatenate(received, axis=join)
 
 
 def make_table(orders, angles):
@@ -41,11 +47,7 @@
     per_device = orders // (snap_size * ord_size)
     shaped = coeffs.reshape(2, ord_size, snap_size * per_device, snap_dev, cycle_count)
     arrived = lax.all_to_all(
-        lax.all_to_all(shaped, "snap", split_axis=2, concat_axis=3, tiled=True),
-        "ord",
-        split_axis=1,
-        concat_axis=3,
-        tiled=True,
+        trade_parts(shaped, "snap", 2, 3), "ord", split_axis=1, concat_axis=3, tiled=True
     )
     arrived = arrived.reshape(2, per_device, -1, cycle_count)
     weight_all = lax.all_gather(weights, "snap", axis=0, tiled=True)

time: 228 us -> 229 us (level)
    reshape x0 -> x1, local copies, waits for them, and re-layouts: none -> 2.53 us  [trade_parts(): return jnp.concatenate(received, axis=join)]
where the time goes in v1:
time: 229 us
  waiting for transfers between devices  106 us (46%)
  blocking collectives  74.8 us (33%)
  between operations  14.2 us (6%)
  matrix products  12.1 us (5%)
  local copies, waits for them, and re-layouts  8.82 us (4%)
  starting transfers between devices  7.41 us (3%)
  other arithmetic  4.87 us (2%)
    reduce_scatter x1, waiting for transfers between devices, on_device(): lax.psum_scatter(partial_count, 'snap', scatter_dimension=0, tiled=True)  68.1 us
    all_to_all x1, blocking collectives, trade_parts(): received = lax.all_to_all(jnp.stack(cells), name, 0, 0)  55.3 us
    all_gather x1, waiting for transfers between devices, on_device(): lax.all_gather(correl, 'ord', axis=0, tiled=True)  33.6 us
    unnamed x1, blocking collectives  19.4 us
    dot_general x1, matrix products, on_device(): jnp.einsum('ka,sqa->ksq', dft_table, images, preferred_element_type=jnp.f...  5.75 us
  transfers between devices with their start and end apart: 4, of which 3 were waited for; matrix products, arithmetic and copies ran while one was open for 1% of the time, Pallas kernels for 0%

profile of v1, /device:TPU:0, one launch (start us, length us, event | category | flops | bytes accessed | tf_op | source)
XLA Modules:
  0.0 228.5 jit_solution(10686810832674885047)
XLA Ops:
  6.5 2.2 multiply_convert_fusion.5
  8.7 0.8 convert_element_type.19
  9.6 5.8 %multiply_convert_fusion.1 = bf16[256,16,256]{2,0,1:T(8,128)(2,1)S(1)} fusion(bf16[16,256,1024]{2,1,0:T(8,128)(2,1)} %param.4, f32[16,256]{1,0:T(8,128)S(1)} %constant_dynamic-slice_fusion, bf16[128,1024]{1,0:T(8,128)(2,1)S(1)} %get-tuple-element.5, bf16[128,1024]{1,0:T(8,128)(2,1)S(1)} %get-tuple-element.6), kind=kOutput, calls=%fused_computation.1 | convolution fusion | flops 2150629376 | bytes 11026432 | tf_op jit(solution)/shard_map/ka,sqa->ksq/dot_general | solution.py:39
  15.3 0.1 fusion.18
  15.5 0.2 fusion.17
  15.6 0.1 fusion.16
  15.8 0.2 fusion.15
  16.0 0.2 fusion.14
  16.1 0.2 fusion.13
  16.3 0.1 fusion.12
  16.5 0.2 fusion.11
  16.6 55.3 %all_to_all.38 = bf16[8,2,4,4,16,256]{5,3,2,1,4,0:T(4,128)(2,1)S(1)} all-to-all(bf16[8,2,4,4,16,256]{5,3,2,1,4,0:T(4,128)(2,1)S(1)} %fusion.11), channel_id=1, replica_groups=mesh['snap'=8,'ord'=4] {'snap'}, dimensions={0} | all-to-all | bytes 4194304 | tf_op jit(solution)/shard_map/all_to_all | solution.py:10
  72.0 2.5 %copy.18 = bf16[2,4,4,8,16,256]{5,4,3,0,2,1:T(8,128)(2,1)} copy(bf16[2,4,4,8,16,256]{5,2,1,0,4,3:T(4,128)(2,1)S(1)} %bitcast.62) | data formatting | bytes 4194304 | tf_op jit(solution)/shard_map/reshape | solution.py:11
  74.5 3.7 %all-to-all-start.1 = ((bf16[2,4,4,128,256]{4,3,0,2,1:T(8,128)(2,1)}), bf16[2,4,4,128,256]{4,3,0,2,1:T(8,128)(2,1)S(1)}, u32[]{:S(2)}, u32[]{:S(2)}) async-start(bf16[2,4,4,128,256]{4,3,0,2,1:T(8,128)(2,1)} %bitcast.61), calls=%async_computation.1 | async-start | bytes 4194304 | tf_op jit(solution)/shard_map/all_to_all | solution.py:49
  78.3 0.6 dynamic-slice
  79.5 0.2 dynamic-update-slice
  79.8 19.4 %all-reduce = f32[512]{0:T(512)S(1)} all-reduce(f32[512]{0:T(512)S(1)} %dynamic-update-slice), channel_id=1, replica_groups=mesh['snap'=8,'ord'=4] {'snap'}, use_global_device_ids=true, to_apply=%add | all-reduce | flops 512 | bytes 4096
  99.2 0.1 reshape.20
  99.4 4.5 %all-to-all-done.1 = bf16[2,4,4,128,256]{4,3,0,2,1:T(8,128)(2,1)S(1)} async-done(((bf16[2,4,4,128,256]{4,3,0,2,1:T(8,128)(2,1)}), bf16[2,4,4,128,256]{4,3,0,2,1:T(8,128)(2,1)S(1)}, u32[]{:S(2)}, u32[]{:S(2)}) %all-to-all-start.1) | async-done | bytes 2097184 | tf_op jit(solution)/shard_map/all_to_all | solution.py:49
  103.9 0.1 copy.19
  104.0 1.2 fusion.2
  105.3 1.6 copy.22
  106.9 3.6 %all-to-all-start.2 = ((f32[4,256,256]{2,0,1:T(4,128)}), f32[4,256,256]{2,0,1:T(4,128)S(1)}, u32[]{:S(2)}, u32[]{:S(2)}) async-start(f32[4,256,256]{2,0,1:T(4,128)} %copy.22), calls=%async_computation.2 | async-start | bytes 2097152 | tf_op jit(solution)/shard_map/all_to_all | solution.py:56
  110.6 1.2 fusion.19
  111.8 68.1 %reduce-scatter.2.cloned.1.call-done = f32[32,256]{1,0:T(8,128)} async-done(((f32[256,256]{1,0:T(8,128)}), f32[32,256]{1,0:T(8,128)}) %reduce-scatter.2.cloned.1.call-update) | async-done | bytes 32784 | tf_op jit(solution)/shard_map/reduce_scatter | solution.py:57
  180.0 0.8 broadcast_maximum_fusion
  180.7 0.3 copy.28
  181.0 0.4 all_to_all.34
  181.4 1.1 broadcast_divide_fusion
  182.5 33.6 %all-gather.2.cloned.1.call-done = f32[128,32,256]{2,0,1:T(8,128)} async-done(((f32[32,32,256]{2,0,1:T(8,128)}), f32[128,32,256]{2,0,1:T(8,128)}) %all-gather.2.cloned.1.call-update) | async-done | bytes 4194320 | tf_op jit(solution)/shard_map/all_gather | solution.py:64
  216.1 4.0 %fusion.22 = f32[32,32,256]{2,0,1:T(8,128)S(1)} fusion(f32[128,32,256]{2,0,1:T(8,128)} %all-gather.2.cloned.1.call-done, f32[128,128]{1,0:T(8,128)S(1)} %copy-done, s32[]{:T(128)S(6)} %select_n.15), kind=kOutput, calls=%fused_computation.40 | convolution fusion | flops 402653184 | bytes 5259268 | tf_op jit(solution)/shard_map/ln,nqp->lqp/dot_general | solution.py:61
  220.1 1.6 copy.24
  (17 shorter events, 0.2 us)
Async XLA Ops:
  6.5 209.6 %copy-start = (f32[128,128]{1,0:T(8,128)S(1)}, f32[128,128]{1,0:T(8,128)}, u32[]{:S(2)}) copy-start(f32[128,128]{1,0:T(8,128)} %param.7) | copy-start | bytes 196612
  74.5 3.8 %copy-start.3 = (u32[32]{0:T(128)S(1)}, u32[32]{0:T(128)}, u32[]{:S(2)}) copy-start(u32[32]{0:T(128)} %constant.37) | copy-start | bytes 388
  74.5 5.0 %copy-start.2 = (f32[64]{0:T(128)S(1)}, f32[64]{0:T(128)}, u32[]{:S(2)}) copy-start(f32[64]{0:T(128)} %param.6) | copy-start | bytes 772
  74.5 29.4 %all-to-all-start.1 = ((bf16[2,4,4,128,256]{4,3,0,2,1:T(8,128)(2,1)}), bf16[2,4,4,128,256]{4,3,0,2,1:T(8,128)(2,1)S(1)}, u32[]{:S(2)}, u32[]{:S(2)}) async-start(bf16[2,4,4,128,256]{4,3,0,2,1:T(8,128)(2,1)} %bitcast.61), calls=%async_computation.1 | async-start | bytes 4194304 | tf_op jit(solution)/shard_map/all_to_all | solution.py:49
  105.3 5.3 %copy-start.1 = (s32[64,256]{1,0:T(8,128)S(1)}, s32[64,256]{1,0:T(8,128)}, u32[]{:S(2)}) copy-start(s32[64,256]{1,0:T(8,128)} %param.5) | copy-start | bytes 196612
  106.9 73.8 %all-to-all-start.2 = ((f32[4,256,256]{2,0,1:T(4,128)}), f32[4,256,256]{2,0,1:T(4,128)S(1)}, u32[]{:S(2)}, u32[]{:S(2)}) async-start(f32[4,256,256]{2,0,1:T(4,128)} %copy.22), calls=%async_computation.2 | async-start | bytes 2097152 | tf_op jit(solution)/shard_map/all_to_all | solution.py:56
  110.5 69.4 %reduce-scatter.2.cloned.1.call-start = ((), (), s32[]{:S(2)}) async-start(), calls=%async_computation.4 | async-start | bytes 294912 | tf_op jit(solution)/shard_map/reduce_scatter | solution.py:57
  111.8 104.3 %all-gather.2.cloned.1.call-start = ((), (), s32[]{:S(2)}) async-start(), calls=%async_computation.5 | async-start | bytes 5242880 | tf_op jit(solution)/shard_map/all_gather | solution.py:64
Sparse Core Ops, SparseCore 0:
  114.7 65.2 reduce-scatter.1
  182.6 33.4 all-gather.1
